TPU v7x, 256 devices: a whole 4x4x8 slice. The times are simulated.
256 devices in a mesh: vox: 64 (over z, x, core), chan: 4 (over y).
Axes of the slice: x: 4, y: 4, z: 8, core: 2. Of those that a mesh axis runs over, the one named last changes fastest.
Arguments:
- model_blocks: bfloat16 [23552, 128, 128], P(('vox', 'chan')), may hold values from -0.15625 to 0.15625
- start_image: float32 [2048, 32, 128], P('vox'), may hold values from 0 to 2
- measured: float32 [2048, 32, 128], P(('vox', 'chan')), may hold values from -6 to 6
- step_size: float32 [32], replicated, may hold values from 0.05 to 0.25
- sent_tiles: int32 [64, 64, 4], P('vox'), may hold values from -1 to 31, as said below
- block_rows: int32 [23552], P(('vox', 'chan')), may hold values from 0 to 7
- block_slots: int32 [23552], P(('vox', 'chan')), may hold values from 0 to 255, as said below
Outputs:
- estimate: float32 [2048, 32, 128], P('vox')
- residual: float32 [2048, 32, 128], P(('vox', 'chan'))
Inputs may be any that keep to these rules, and one draw needn't show every extreme that they name: `sent_tiles`: an entry is -1 for an unused slot, else a tile of slab j; the used slots of one pair (j, v) come first, hold distinct tiles, number 1 to 4, and slab v always uses all 4 slots for itself. `block_slots`: every block names a used slot of its own device's vox index v, that is sent_tiles[j, v, s] is not -1.
All inputs are finite; a program needn't handle non-finite values.
Results may differ from a plain program's by a relative error of at most 0.0045.
Values may be sent and summed in bfloat16 or wider, within the bound.
A program may use at most 64 MiB of HBM per device.

v0:
```python
import jax
import jax.numpy as jnp
from jax import lax
from jax.sharding import PartitionSpec as P

ITERATIONS = 4


def shards(model_blocks, start_image, measured, step_size, sent_tiles, block_rows, block_slots):
    vox_count = lax.axis_size("vox")
    send_table = sent_tiles[0]
    capacity = send_table.shape[1]
    tile_count = start_image.shape[0]
    wave_count = start_image.shape[1]
    block_width = start_image.shape[2]
    row_count = measured.shape[0]
    block_count = model_blocks.shape[0]
    row_hot = (block_rows[None, :] == jnp.arange(row_count, dtype=jnp.int32)[:, None]).astype(
        jnp.float32
    )
    slot_hot = (
        block_slots[None, :] == jnp.arange(vox_count * capacity, dtype=jnp.int32)[:, None]
    ).astype(jnp.float32)
    tile_range = jnp.arange(tile_count, dtype=jnp.int32)[:, None]
    return_hot = (send_table.reshape(1, -1) == tile_range).astype(jnp.float32)
    step_gains = step_size[None, :, None]
    estimate = start_image
    residual = measured
    for iteration in range(ITERATIONS):
        rounded = estimate.astype(jnp.bfloat16)
        outgoing = jnp.take(rounded, jnp.maximum(send_table, 0), axis=0)
        arrived = lax.all_to_all(outgoing, "vox", split_axis=0, concat_axis=0, tiled=True)
        flat_tiles = arrived.reshape(vox_count * capacity, wave_count, block_width)
        forward_picked = jnp.take(flat_tiles, block_slots, axis=0)
        products = jnp.einsum(
            "bwv,bsv->bws", forward_picked, model_blocks, preferred_element_type=jnp.float32
        )
        summed = jnp.dot(
            row_hot,
            products.reshape(block_count, wave_count * block_width),
            precision=lax.Precision.HIGHEST,
        )
        residual = measured - summed.reshape(row_count, wave_count, block_width)
        narrow = residual.astype(jnp.bfloat16)
        picked = jnp.take(narrow, block_rows, axis=0)
        adjoint_terms = jnp.einsum(
            "bws,bsv->bwv", picked, model_blocks, preferred_element_type=jnp.float32
        )
        slot_sums = jnp.dot(
            slot_hot,
            adjoint_terms.reshape(block_count, wave_count * block_width),
            precision=lax.Precision.HIGHEST,
        )
        slot_sums = slot_sums.reshape(vox_count, capacity, wave_count, block_width)
        returned = lax.all_to_all(slot_sums, "vox", split_axis=0, concat_axis=0, tiled=True)
        local_sum = jnp.dot(
            return_hot,
            returned.reshape(-1, wave_count * block_width),
            precision=lax.Precision.HIGHEST,
        )
        slab_total = lax.psum(local_sum, "chan")
        estimate = jnp.maximum(
            estimate + step_gains * slab_total.reshape(tile_count, wave_count, block_width), 0.0
        )
    return (estimate, residual)


def solution(mesh):
    in_specs = (
        P(("vox", "chan"), None, None),
        P("vox", None, None),
        P(("vox", "chan"), None, None),
        P(),
        P("vox", None, None),
        P(("vox", "chan")),
        P(("vox", "chan")),
    )
    out_specs = (P("vox", None, None), P(("vox", "chan"), None, None))
    return jax.shard_map(shards, mesh=mesh, in_specs=in_specs, out_specs=out_specs, check_vma=False)
```

profile of v0, /device:TPU:2, one launch (start us, length us, event | category | flops | bytes accessed | tf_op | source)
XLA Modules:
  0.0 964.7 jit_solution(2402718531708179896)
XLA Ops:
  10.2 2.2 gather_fusion
  12.4 2.7 broadcast_select_fusion.3
  15.1 12.3 %all-to-all-start = ((bf16[64,4,32,128]{3,2,1,0:T(8,128)(2,1)}), bf16[64,4,32,128]{3,2,1,0:T(8,128)(2,1)}, u32[]{:S(2)}, u32[]{:S(2)}) async-start(bf16[64,4,32,128]{3,2,1,0:T(8,128)(2,1)} %broadcast_select_fusion.3), calls=%async_computation | async-start | bytes 4194304 | tf_op jit(solution)/shard_map/all_to_all | solution.py:32
  27.6 51.0 %all-to-all-done = bf16[64,4,32,128]{3,2,1,0:T(8,128)(2,1)} async-done(((bf16[64,4,32,128]{3,2,1,0:T(8,128)(2,1)}), bf16[64,4,32,128]{3,2,1,0:T(8,128)(2,1)}, u32[]{:S(2)}, u32[]{:S(2)}) %all-to-all-start) | async-done | bytes 2097184 | tf_op jit(solution)/shard_map/all_to_all | solution.py:32
  78.6 3.1 gather_fusion.1
  81.8 2.8 fusion.79
  88.6 2.1 fusion.77
  90.8 2.6 fusion.18
  93.4 4.4 copy.71
  97.8 6.2 all-to-all-start.1
  104.3 95.7 %all-to-all-done.1 = f32[64,4,32,128]{3,2,1,0:T(8,128)} async-done(((f32[64,4,32,128]{3,2,1,0:T(8,128)}), f32[64,4,32,128]{3,2,1,0:T(8,128)}, u32[]{:S(2)}, u32[]{:S(2)}) %all-to-all-start.1) | async-done | bytes 4194336 | tf_op jit(solution)/shard_map/all_to_all | solution.py:55
  200.0 5.9 fusion.32
  206.8 44.8 %all-reduce.5.cloned.1.call-done = f32[32,32,128]{2,1,0:T(8,128)} async-done(((f32[32,32,128]{2,1,0:T(8,128)}), f32[32,32,128]{2,1,0:T(8,128)}) %all-reduce.5.cloned.1.call-update) | async-done | bytes 524304 | tf_op jit(solution)/shard_map/psum | solution.py:61
  253.0 2.2 gather_fusion.3
  255.2 1.8 broadcast_select_fusion.2
  256.9 61.7 %all_to_all.40 = bf16[64,4,32,128]{3,2,1,0:T(8,128)(2,1)} all-to-all(bf16[64,4,32,128]{3,2,1,0:T(8,128)(2,1)S(1)} %broadcast_select_fusion.2), channel_id=1, replica_groups=mesh['vox'=64,'chan'=4] {'vox'}, dimensions={0} | all-to-all | bytes 4194304 | tf_op jit(solution)/shard_map/all_to_all | solution.py:32
  318.6 3.1 gather_fusion.4
  321.8 2.8 fusion.75
  327.8 2.1 fusion.73
  330.0 2.6 fusion.16
  332.6 2.4 copy.78
  335.1 101.8 %all_to_all.41 = f32[64,4,32,128]{3,2,1,0:T(8,128)S(1)} all-to-all(f32[64,4,32,128]{3,2,1,0:T(8,128)S(1)} %copy.78), channel_id=1, replica_groups=mesh['vox'=64,'chan'=4] {'vox'}, dimensions={0} | all-to-all | bytes 8388608 | tf_op jit(solution)/shard_map/all_to_all | solution.py:55
  436.9 3.9 fusion.35
  441.8 43.9 %all-reduce.7.cloned.1.call-done = f32[32,32,128]{2,1,0:T(8,128)} async-done(((f32[32,32,128]{2,1,0:T(8,128)}), f32[32,32,128]{2,1,0:T(8,128)}) %all-reduce.7.cloned.1.call-update) | async-done | bytes 524304 | tf_op jit(solution)/shard_map/psum | solution.py:61
  485.7 2.4 fusion.136
  488.0 2.2 gather_fusion.6
  490.2 1.8 broadcast_select_fusion.1
  492.0 61.8 %all_to_all.42 = bf16[64,4,32,128]{3,2,1,0:T(8,128)(2,1)} all-to-all(bf16[64,4,32,128]{3,2,1,0:T(8,128)(2,1)S(1)} %broadcast_select_fusion.1), channel_id=1, replica_groups=mesh['vox'=64,'chan'=4] {'vox'}, dimensions={0} | all-to-all | bytes 4194304 | tf_op jit(solution)/shard_map/all_to_all | solution.py:32
  553.8 3.1 gather_fusion.7
  557.0 2.8 fusion.71
  563.0 2.1 fusion.69
  565.2 2.6 fusion.14
  567.9 2.4 copy.85
  570.3 101.6 %all_to_all.43 = f32[64,4,32,128]{3,2,1,0:T(8,128)S(1)} all-to-all(f32[64,4,32,128]{3,2,1,0:T(8,128)S(1)} %copy.85), channel_id=1, replica_groups=mesh['vox'=64,'chan'=4] {'vox'}, dimensions={0} | all-to-all | bytes 8388608 | tf_op jit(solution)/shard_map/all_to_all | solution.py:55
  671.9 3.9 fusion.38
  676.8 43.9 %all-reduce.9.cloned.1.call-done = f32[32,32,128]{2,1,0:T(8,128)} async-done(((f32[32,32,128]{2,1,0:T(8,128)}), f32[32,32,128]{2,1,0:T(8,128)}) %all-reduce.9.cloned.1.call-update) | async-done | bytes 524304 | tf_op jit(solution)/shard_map/psum | solution.py:61
  722.0 2.2 gather_fusion.9
  726.0 61.9 %all_to_all.44 = bf16[64,4,32,128]{3,2,1,0:T(8,128)(2,1)} all-to-all(bf16[64,4,32,128]{3,2,1,0:T(8,128)(2,1)S(1)} %broadcast_select_fusion), channel_id=1, replica_groups=mesh['vox'=64,'chan'=4] {'vox'}, dimensions={0} | all-to-all | bytes 4194304 | tf_op jit(solution)/shard_map/all_to_all | solution.py:32
  787.9 3.1 gather_fusion.10
  791.1 2.8 fusion.67
  794.0 2.1 fusion.137
  797.7 2.1 fusion.65
  799.9 2.6 fusion.12
  802.6 2.4 copy.92
  805.0 101.7 %all_to_all.45 = f32[64,4,32,128]{3,2,1,0:T(8,128)S(1)} all-to-all(f32[64,4,32,128]{3,2,1,0:T(8,128)S(1)} %copy.92), channel_id=1, replica_groups=mesh['vox'=64,'chan'=4] {'vox'}, dimensions={0} | all-to-all | bytes 8388608 | tf_op jit(solution)/shard_map/all_to_all | solution.py:55
  906.7 3.9 fusion.41
  913.1 42.3 %all-reduce.11.cloned.1.call-done = f32[32,32,128]{2,1,0:T(8,128)} async-done(((f32[32,32,128]{2,1,0:T(8,128)}), f32[32,32,128]{2,1,0:T(8,128)}) %all-reduce.11.cloned.1.call-update) | async-done | bytes 524304 | tf_op jit(solution)/shard_map/psum | solution.py:61
  955.5 2.2 add_maximum_fusion
  (65 shorter events, 25.6 us)
Async XLA Ops:
  7.2 74.6 %copy-start = (bf16[92,128,128]{2,1,0:T(8,128)(2,1)S(1)}, bf16[92,128,128]{2,1,0:T(8,128)(2,1)}, u32[]{:S(2)}) copy-start(bf16[92,128,128]{2,1,0:T(8,128)(2,1)} %param.13) | copy-start | bytes 9043972
  15.1 12.4 %copy-start.4 = (s32[92]{0:T(128)S(1)}, s32[92]{0:T(128)}, u32[]{:S(2)}) copy-start(s32[92]{0:T(128)} %param.19) | copy-start | bytes 1108
  15.1 12.4 %copy-start.6 = (s32[92]{0:T(128)S(1)}, s32[92]{0:T(128)}, u32[]{:S(2)}) copy-start(s32[92]{0:T(128)} %param.18) | copy-start | bytes 1108
  15.1 63.5 %all-to-all-start = ((bf16[64,4,32,128]{3,2,1,0:T(8,128)(2,1)}), bf16[64,4,32,128]{3,2,1,0:T(8,128)(2,1)}, u32[]{:S(2)}, u32[]{:S(2)}) async-start(bf16[64,4,32,128]{3,2,1,0:T(8,128)(2,1)} %broadcast_select_fusion.3), calls=%async_computation | async-start | bytes 4194304 | tf_op jit(solution)/shard_map/all_to_all | solution.py:32
  84.6 0.9 copy-start.2
  97.8 6.2 copy-start.3
  97.8 102.1 %all-to-all-start.1 = ((f32[64,4,32,128]{3,2,1,0:T(8,128)}), f32[64,4,32,128]{3,2,1,0:T(8,128)}, u32[]{:S(2)}, u32[]{:S(2)}) async-start(f32[64,4,32,128]{3,2,1,0:T(8,128)} %copy.71), calls=%async_computation.1 | async-start | bytes 8388608 | tf_op jit(solution)/shard_map/all_to_all | solution.py:55
  104.0 147.6 %all-reduce.5.cloned.1.call-start = ((), (), s32[]{:S(2)}) async-start(), calls=%async_computation.8 | async-start | bytes 1048576 | tf_op jit(solution)/shard_map/psum | solution.py:61
  200.0 51.7 %copy-start.5 = (f32[32]{0:T(128)S(1)}, f32[32]{0:T(128)}, u32[]{:S(2)}) copy-start(f32[32]{0:T(128)} %param.16) | copy-start | bytes 388
  206.8 278.9 %all-reduce.7.cloned.1.call-start = ((), (), s32[]{:S(2)}) async-start(), calls=%async_computation.9 | async-start | bytes 1048576 | tf_op jit(solution)/shard_map/psum | solution.py:61
  441.7 278.9 %all-reduce.9.cloned.1.call-start = ((), (), s32[]{:S(2)}) async-start(), calls=%async_computation.10 | async-start | bytes 1048576 | tf_op jit(solution)/shard_map/psum | solution.py:61
  676.8 278.7 %all-reduce.11.cloned.1.call-start = ((), (), s32[]{:S(2)}) async-start(), calls=%async_computation.11 | async-start | bytes 1048576 | tf_op jit(solution)/shard_map/psum | solution.py:61
  910.6 44.8 %copy-start.1 = (f32[32,32,128]{2,1,0:T(8,128)S(1)}, f32[32,32,128]{2,1,0:T(8,128)}, u32[]{:S(2)}) copy-start(f32[32,32,128]{2,1,0:T(8,128)} %get-tuple-element.14) | copy-start | bytes 1572868
Sparse Core Ops, SparseCore 0:
  206.9 44.6 all-reduce.4
  441.8 43.7 all-reduce.6
  676.9 43.7 all-reduce.8
  911.7 43.7 all-reduce.10
where the time goes:
time: 974 us; the launch traced here: 965 us
  blocking collectives  491 us (50%)
  waiting for transfers between devices  322 us (33%)
  matrix products  54.4 us (6%)
  local copies, waits for them, and re-layouts  46.8 us (5%)
  starting transfers between devices  18.7 us (2%)
  other arithmetic  18.1 us (2%)
  between operations  14.6 us (1%)
    all_to_all x3, blocking collectives, shards(): lax.all_to_all(slot_sums, 'vox', split_axis=0, concat_axis=0, tiled=True)  305 us
    all_to_all x3, blocking collectives, shards(): lax.all_to_all(outgoing, 'vox', split_axis=0, concat_axis=0, tiled=True)  185 us
    psum x4, waiting for transfers between devices, shards(): slab_total = lax.psum(local_sum, 'chan')  175 us
    all_to_all x1, waiting for transfers between devices, shards(): lax.all_to_all(slot_sums, 'vox', split_axis=0, concat_axis=0, tiled=True)  95.7 us
    all_to_all x1, waiting for transfers between devices, shards(): lax.all_to_all(outgoing, 'vox', split_axis=0, concat_axis=0, tiled=True)  51 us
  transfers between devices with their start and end apart: 6, of which 6 were waited for; matrix products, arithmetic and copies ran while one was open for 0% of the time, Pallas kernels for 0%

commit v1 on v0

--- a/solution.py
+++ b/solution.py
@@ -58,7 +58,7 @@
             returned.reshape(-1, wave_count * block_width),
             precision=lax.Precision.HIGHEST,
         )
-        slab_total = lax.psum(local_sum, "chan")
+        slab_total = jnp.sum(lax.all_gather(local_sum, "chan"), axis=0)
         estimate = jnp.maximum(
             estimate + step_gains * slab_total.reshape(tile_count, wave_count, block_width), 0.0
         )

time: 974 us -> 929 us (0.954)
  waiting for transfers between devices: 322 us -> 260 us
    psum x4 -> x0, waiting for transfers between devices: 175 us -> none  [shards(): slab_total = lax.psum(local_sum, 'chan')]
    all_gather x0 -> x4, waiting for transfers between devices: none -> 113 us  [shards(): slab_total = jnp.sum(lax.all_gather(local_sum, 'chan'), axis=0)]
    reduce_sum x0 -> x4, other arithmetic: none -> 10.2 us  [shards(): slab_total = jnp.sum(lax.all_gather(local_sum, 'chan'), axis=0)]
where the time goes in v1:
time: 929 us; the launch traced here: 919 us
  blocking collectives  491 us (53%)
  waiting for transfers between devices  260 us (28%)
  matrix products  57.5 us (6%)
  local copies, waits for them, and re-layouts  49.5 us (5%)
  other arithmetic  27.7 us (3%)
  starting transfers between devices  18.7 us (2%)
  between operations  14.6 us (2%)
    all_to_all x3, blocking collectives, shards(): lax.all_to_all(slot_sums, 'vox', split_axis=0, concat_axis=0, tiled=True)  305 us
    all_to_all x3, blocking collectives, shards(): lax.all_to_all(outgoing, 'vox', split_axis=0, concat_axis=0, tiled=True)  185 us
    all_gather x4, waiting for transfers between devices, shards(): slab_total = jnp.sum(lax.all_gather(local_sum, 'chan'), axis=0)  113 us
    all_to_all x1, waiting for transfers between devices, shards(): lax.all_to_all(slot_sums, 'vox', split_axis=0, concat_axis=0, tiled=True)  95.7 us
    all_to_all x1, waiting for transfers between devices, shards(): lax.all_to_all(outgoing, 'vox', split_axis=0, concat_axis=0, tiled=True)  51 us
    dot_general x4, matrix products, shards(): jnp.dot(return_hot, returned.reshape(-1, wave_count * block_width), preci...  20.8 us
  transfers between devices with their start and end apart: 6, of which 6 were waited for; matrix products, arithmetic and copies ran while one was open for 0% of the time, Pallas kernels for 0%

profile of v1, /device:TPU:2, one launch (start us, length us, event | category | flops | bytes accessed | tf_op | source)
XLA Modules:
  0.0 918.7 jit_solution(10555054789632295731)
XLA Ops:
  10.2 2.2 gather_fusion
  12.4 2.8 broadcast_select_fusion.3
  15.1 12.3 %all-to-all-start = ((bf16[64,4,32,128]{3,2,1,0:T(8,128)(2,1)}), bf16[64,4,32,128]{3,2,1,0:T(8,128)(2,1)}, u32[]{:S(2)}, u32[]{:S(2)}) async-start(bf16[64,4,32,128]{3,2,1,0:T(8,128)(2,1)} %broadcast_select_fusion.3), calls=%async_computation | async-start | bytes 4194304 | tf_op jit(solution)/shard_map/all_to_all | solution.py:32
  27.6 51.0 %all-to-all-done = bf16[64,4,32,128]{3,2,1,0:T(8,128)(2,1)} async-done(((bf16[64,4,32,128]{3,2,1,0:T(8,128)(2,1)}), bf16[64,4,32,128]{3,2,1,0:T(8,128)(2,1)}, u32[]{:S(2)}, u32[]{:S(2)}) %all-to-all-start) | async-done | bytes 2097184 | tf_op jit(solution)/shard_map/all_to_all | solution.py:32
  78.6 3.2 gather_fusion.1
  81.8 2.8 fusion.67
  88.6 2.1 fusion.65
  90.8 2.6 fusion.18
  93.5 4.4 copy.71
  97.9 6.2 all-to-all-start.1
  104.3 95.7 %all-to-all-done.1 = f32[64,4,32,128]{3,2,1,0:T(8,128)} async-done(((f32[64,4,32,128]{3,2,1,0:T(8,128)}), f32[64,4,32,128]{3,2,1,0:T(8,128)}, u32[]{:S(2)}, u32[]{:S(2)}) %all-to-all-start.1) | async-done | bytes 4194336 | tf_op jit(solution)/shard_map/all_to_all | solution.py:55
  200.0 6.7 fusion.9
  206.7 29.8 %all-gather.9.cloned.1.call-done = f32[128,4096]{1,0:T(8,128)} async-done(((f32[32,4096]{1,0:T(8,128)}), f32[128,4096]{1,0:T(8,128)}) %all-gather.9.cloned.1.call-update) | async-done | bytes 2097168 | tf_op jit(solution)/shard_map/all_gather | solution.py:61
  236.5 2.5 reduce_sum.36
  242.2 2.2 gather_fusion.3
  246.2 61.7 %all_to_all.40 = bf16[64,4,32,128]{3,2,1,0:T(8,128)(2,1)} all-to-all(bf16[64,4,32,128]{3,2,1,0:T(8,128)(2,1)S(1)} %broadcast_select_fusion.2), channel_id=1, replica_groups=mesh['vox'=64,'chan'=4] {'vox'}, dimensions={0} | all-to-all | bytes 4194304 | tf_op jit(solution)/shard_map/all_to_all | solution.py:32
  307.9 3.2 gather_fusion.4
  311.0 2.8 fusion.63
  317.1 2.1 fusion.61
  319.3 2.6 fusion.16
  321.9 2.4 copy.78
  324.3 101.8 %all_to_all.41 = f32[64,4,32,128]{3,2,1,0:T(8,128)S(1)} all-to-all(f32[64,4,32,128]{3,2,1,0:T(8,128)S(1)} %copy.78), channel_id=1, replica_groups=mesh['vox'=64,'chan'=4] {'vox'}, dimensions={0} | all-to-all | bytes 8388608 | tf_op jit(solution)/shard_map/all_to_all | solution.py:55
  426.1 4.7 fusion.6
  430.9 28.4 %all-gather.11.cloned.1.call-done = f32[128,4096]{1,0:T(8,128)} async-done(((f32[32,4096]{1,0:T(8,128)}), f32[128,4096]{1,0:T(8,128)}) %all-gather.11.cloned.1.call-update) | async-done | bytes 2097168 | tf_op jit(solution)/shard_map/all_gather | solution.py:61
  459.3 2.5 reduce_sum.37
  463.0 2.2 fusion.132
  465.2 2.2 gather_fusion.6
  469.2 61.8 %all_to_all.42 = bf16[64,4,32,128]{3,2,1,0:T(8,128)(2,1)} all-to-all(bf16[64,4,32,128]{3,2,1,0:T(8,128)(2,1)S(1)} %broadcast_select_fusion.1), channel_id=1, replica_groups=mesh['vox'=64,'chan'=4] {'vox'}, dimensions={0} | all-to-all | bytes 4194304 | tf_op jit(solution)/shard_map/all_to_all | solution.py:32
  531.0 3.2 gather_fusion.7
  534.2 2.8 fusion.59
  540.2 2.1 fusion.57
  542.4 2.6 fusion.14
  545.1 2.4 copy.85
  547.5 101.6 %all_to_all.43 = f32[64,4,32,128]{3,2,1,0:T(8,128)S(1)} all-to-all(f32[64,4,32,128]{3,2,1,0:T(8,128)S(1)} %copy.85), channel_id=1, replica_groups=mesh['vox'=64,'chan'=4] {'vox'}, dimensions={0} | all-to-all | bytes 8388608 | tf_op jit(solution)/shard_map/all_to_all | solution.py:55
  649.1 4.7 fusion.3
  653.9 28.4 %all-gather.13.cloned.1.call-done = f32[128,4096]{1,0:T(8,128)} async-done(((f32[32,4096]{1,0:T(8,128)}), f32[128,4096]{1,0:T(8,128)}) %all-gather.13.cloned.1.call-update) | async-done | bytes 2097168 | tf_op jit(solution)/shard_map/all_gather | solution.py:61
  682.3 2.6 reduce_sum.38
  688.0 2.2 gather_fusion.9
  692.0 61.9 %all_to_all.44 = bf16[64,4,32,128]{3,2,1,0:T(8,128)(2,1)} all-to-all(bf16[64,4,32,128]{3,2,1,0:T(8,128)(2,1)S(1)} %broadcast_select_fusion), channel_id=1, replica_groups=mesh['vox'=64,'chan'=4] {'vox'}, dimensions={0} | all-to-all | bytes 4194304 | tf_op jit(solution)/shard_map/all_to_all | solution.py:32
  753.9 3.2 gather_fusion.10
  757.0 2.8 fusion.55
  760.0 2.1 fusion.134
  765.9 2.6 fusion.12
  768.6 2.4 copy.92
  771.0 101.7 %all_to_all.45 = f32[64,4,32,128]{3,2,1,0:T(8,128)S(1)} all-to-all(f32[64,4,32,128]{3,2,1,0:T(8,128)S(1)} %copy.92), channel_id=1, replica_groups=mesh['vox'=64,'chan'=4] {'vox'}, dimensions={0} | all-to-all | bytes 8388608 | tf_op jit(solution)/shard_map/all_to_all | solution.py:55
  872.7 4.7 fusion
  879.1 26.8 %all-gather.15.cloned.1.call-done = f32[128,4096]{1,0:T(8,128)} async-done(((f32[32,4096]{1,0:T(8,128)}), f32[128,4096]{1,0:T(8,128)}) %all-gather.15.cloned.1.call-update) | async-done | bytes 2097168 | tf_op jit(solution)/shard_map/all_gather | solution.py:61
  905.9 2.6 reduce_sum.39
  (73 shorter events, 35.6 us)
Async XLA Ops:
  7.2 74.6 %copy-start = (bf16[92,128,128]{2,1,0:T(8,128)(2,1)S(1)}, bf16[92,128,128]{2,1,0:T(8,128)(2,1)}, u32[]{:S(2)}) copy-start(bf16[92,128,128]{2,1,0:T(8,128)(2,1)} %param.13) | copy-start | bytes 9043972
  15.1 12.4 %copy-start.6 = (s32[92]{0:T(128)S(1)}, s32[92]{0:T(128)}, u32[]{:S(2)}) copy-start(s32[92]{0:T(128)} %param.19) | copy-start | bytes 1108
  15.1 12.4 %copy-start.8 = (s32[92]{0:T(128)S(1)}, s32[92]{0:T(128)}, u32[]{:S(2)}) copy-start(s32[92]{0:T(128)} %param.18) | copy-start | bytes 1108
  15.1 63.5 %all-to-all-start = ((bf16[64,4,32,128]{3,2,1,0:T(8,128)(2,1)}), bf16[64,4,32,128]{3,2,1,0:T(8,128)(2,1)}, u32[]{:S(2)}, u32[]{:S(2)}) async-start(bf16[64,4,32,128]{3,2,1,0:T(8,128)(2,1)} %broadcast_select_fusion.3), calls=%async_computation | async-start | bytes 4194304 | tf_op jit(solution)/shard_map/all_to_all | solution.py:32
  84.6 0.9 copy-start.4
  97.8 6.2 copy-start.5
  97.9 102.1 %all-to-all-start.1 = ((f32[64,4,32,128]{3,2,1,0:T(8,128)}), f32[64,4,32,128]{3,2,1,0:T(8,128)}, u32[]{:S(2)}, u32[]{:S(2)}) async-start(f32[64,4,32,128]{3,2,1,0:T(8,128)} %copy.71), calls=%async_computation.1 | async-start | bytes 8388608 | tf_op jit(solution)/shard_map/all_to_all | solution.py:55
  104.0 132.5 %all-gather.9.cloned.1.call-start = ((), (), s32[]{:S(2)}) async-start(), calls=%async_computation.8 | async-start | bytes 2621440 | tf_op jit(solution)/shard_map/all_gather | solution.py:61
  206.6 34.4 %copy-start.7 = (f32[32]{0:T(128)S(1)}, f32[32]{0:T(128)}, u32[]{:S(2)}) copy-start(f32[32]{0:T(128)} %param.16) | copy-start | bytes 388
  206.7 252.7 %all-gather.11.cloned.1.call-start = ((), (), s32[]{:S(2)}) async-start(), calls=%async_computation.9 | async-start | bytes 2621440 | tf_op jit(solution)/shard_map/all_gather | solution.py:61
  240.2 0.8 copy-start.3
  430.9 251.4 %all-gather.13.cloned.1.call-start = ((), (), s32[]{:S(2)}) async-start(), calls=%async_computation.10 | async-start | bytes 2621440 | tf_op jit(solution)/shard_map/all_gather | solution.py:61
  653.9 252.0 %all-gather.15.cloned.1.call-start = ((), (), s32[]{:S(2)}) async-start(), calls=%async_computation.11 | async-start | bytes 2621440 | tf_op jit(solution)/shard_map/all_gather | solution.py:61
  686.0 0.8 copy-start.2
  877.5 32.1 %copy-start.1 = (f32[32,32,128]{2,1,0:T(8,128)S(1)}, f32[32,32,128]{2,1,0:T(8,128)}, u32[]{:S(2)}) copy-start(f32[32,32,128]{2,1,0:T(8,128)} %get-tuple-element.14) | copy-start | bytes 1572868
Sparse Core Ops, SparseCore 0:
  206.8 29.7 all-gather.8
  431.0 28.2 all-gather.10
  654.0 28.2 all-gather.12
  877.6 28.2 all-gather.14
